TPU v7x, 128 devices: a whole 4x4x4 slice. The times are simulated.
128 devices in a mesh: ctx: 16 (over x, z), head: 8 (over y, core).
Axes of the slice: x: 4, y: 4, z: 4, core: 2. Of those that a mesh axis runs over, the one named last changes fastest.
Arguments:
- queries: bfloat16 [64, 8192], P('ctx', 'head'), may hold values from -16 to 16
- keys: bfloat16 [524288, 8, 128], P('ctx', 'head'), may hold values from -16 to 16
- values: bfloat16 [524288, 8, 128], P('ctx', 'head'), may hold values from -4 to 4
- offsets: int32 [16], P('ctx'), may hold values from 0 to 491520, as said below
- lengths: int32 [64], replicated, may hold values from 262144 to 524288
- residual: bfloat16 [64, 5120], P(None, 'ctx'), may hold values from -2 to 2
- wo: bfloat16 [8192, 5120], P('head', 'ctx'), may hold values from -0.0625 to 0.0625
- norm_gain: float32 [5120], P('ctx'), may hold values from 0.1 to 1.9
- w_gate: bfloat16 [5120, 25600], P('ctx', 'head'), may hold values from -0.078125 to 0.078125
- w_up: bfloat16 [5120, 25600], P('ctx', 'head'), may hold values from -0.078125 to 0.078125
- w_down: bfloat16 [25600, 5120], P('head', 'ctx'), may hold values from -0.0390625 to 0.0390625
Outputs:
- attended: bfloat16 [64, 8192], P('ctx', 'head')
- stream: bfloat16 [64, 5120], P(None, 'ctx')
- ffn_out: bfloat16 [64, 5120], P('head', 'ctx')
Inputs may be any that keep to these rules, and one draw needn't show every extreme that they name: offsets holds each of 0, 32768, ..., 491520 once.
All inputs are finite; a program needn't handle non-finite values.
Results may differ from a plain program's by a relative error of at most 0.02.
Values may be sent and summed in bfloat16 or wider, within the bound.
A program may use at most 128 MiB of HBM per device.

v0:
```python
import math
import jax
import jax.numpy as jnp
from jax import lax
from jax.sharding import PartitionSpec as P

D = 5120
masked_score = -1e30
epsilon = 1e-06


def activate(gate, upward, square_total):
    scale = lax.rsqrt(square_total / D + epsilon)[:, None]
    return (jax.nn.silu(scale * gate) * (scale * upward)).astype(jnp.bfloat16)


def local(queries, keys, values, offsets, lengths, residual, wo, norm_gain, w_gate, w_up, w_down):
    head_size = keys.shape[2]
    kv_local = keys.shape[1]
    rows_local = queries.shape[0]
    everyone = lax.all_gather(queries, "ctx", axis=0, tiled=True)
    batch = everyone.shape[0]
    groups = everyone.shape[1] // (kv_local * head_size)
    query_heads = everyone.reshape(batch, kv_local, groups, head_size)
    query_heads = query_heads.transpose(1, 0, 2, 3).reshape(kv_local, batch * groups, head_size)
    row_limit = jnp.repeat(lengths, groups)
    inverse_root = 1.0 / math.sqrt(head_size)
    span = keys.shape[0]
    block = min(2048, span)
    turns = span // block
    shard_begin = offsets[0]

    def visit(carry, block_index):
        row_high, row_total, row_acc = carry
        first_slot = block_index * block
        key_block = lax.dynamic_slice_in_dim(keys, first_slot, block, 0)
        value_block = lax.dynamic_slice_in_dim(values, first_slot, block, 0)
        scores = (
            jnp.einsum("hrd,khd->hrk", query_heads, key_block, preferred_element_type=jnp.float32)
            * inverse_root
        )
        position = shard_begin + first_slot + jnp.arange(block, dtype=jnp.int32)
        scores = jnp.where(position[None, None, :] < row_limit[None, :, None], scores, masked_score)
        new_high = jnp.maximum(row_high, jnp.max(scores, axis=2))
        weights = jnp.exp(scores - new_high[:, :, None])
        rescale = jnp.exp(row_high - new_high)
        row_total = row_total * rescale + jnp.sum(weights, axis=2)
        update = jnp.einsum(
            "hrk,khd->hrd",
            weights.astype(jnp.bfloat16),
            value_block,
            preferred_element_type=jnp.float32,
        )
        row_acc = row_acc * rescale[:, :, None] + update
        return ((new_high, row_total, row_acc), None)

    start_high = jnp.full((kv_local, batch * groups), masked_score, jnp.float32)
    start_total = jnp.zeros((kv_local, batch * groups), jnp.float32)
    start_acc = jnp.zeros((kv_local, batch * groups, head_size), jnp.float32)
    (row_high, row_total, row_acc), _ = lax.scan(
        visit, (start_high, start_total, start_acc), jnp.arange(turns, dtype=jnp.int32)
    )
    heads_local = kv_local * groups
    row_high = (
        row_high.reshape(kv_local, batch, groups).transpose(1, 0, 2).reshape(batch, heads_local)
    )
    row_total = (
        row_total.reshape(kv_local, batch, groups).transpose(1, 0, 2).reshape(batch, heads_local)
    )
    row_acc = (
        row_acc.reshape(kv_local, batch, groups, head_size)
        .transpose(1, 0, 2, 3)
        .reshape(batch, heads_local, head_size)
    )
    top_score = lax.pmax(row_high, "ctx")
    rescale = jnp.exp(row_high - top_score)
    summed_acc, summed_total = lax.psum((row_acc * rescale[:, :, None], row_total * rescale), "ctx")
    whole_rows = (
        (summed_acc / summed_total[:, :, None])
        .reshape(batch, heads_local * head_size)
        .astype(jnp.bfloat16)
    )
    attended = lax.dynamic_slice_in_dim(
        whole_rows, lax.axis_index("ctx") * rows_local, rows_local, 0
    )
    projected = jnp.dot(whole_rows, wo, preferred_element_type=jnp.float32)
    mixed = lax.psum(projected, "head")
    combined = residual.astype(jnp.float32) + mixed
    stream = combined.astype(jnp.bfloat16)
    squares = jnp.sum(combined * combined, axis=1)
    normed = (combined * norm_gain).astype(jnp.bfloat16)
    gate_part = jnp.dot(normed, w_gate, preferred_element_type=jnp.float32)
    up_part = jnp.dot(normed, w_up, preferred_element_type=jnp.float32)
    square_total = lax.psum(squares, "ctx")
    gate, upward = lax.psum((gate_part, up_part), "ctx")
    hidden = activate(gate, upward, square_total)
    ffn_out = lax.psum_scatter(
        jnp.dot(hidden, w_down, preferred_element_type=jnp.float32),
        "head",
        scatter_dimension=0,
        tiled=True,
    ).astype(jnp.bfloat16)
    return (attended, stream, ffn_out)


def solution(mesh):
    return jax.shard_map(
        local,
        mesh=mesh,
        in_specs=(
            P("ctx", "head"),
            P("ctx", "head", None),
            P("ctx", "head", None),
            P("ctx"),
            P(),
            P(None, "ctx"),
            P("head", "ctx"),
            P("ctx"),
            P("ctx", "head"),
            P("ctx", "head"),
            P("head", "ctx"),
        ),
        out_specs=(P("ctx", "head"), P(None, "ctx"), P("head", "ctx")),
        check_vma=False,
    )
```

profile of v0, /device:TPU:0, one launch (start us, length us, event | category | flops | bytes accessed | tf_op | source)
XLA Modules:
  0.0 567.2 jit_solution(13764307791366499281)
XLA Ops:
  7.3 25.3 %all-gather = bf16[16,4,1024]{2,1,0:T(4,128)(2,1)S(1)} all-gather(bf16[1,4,1024]{2,1,0:T(4,128)(2,1)} %bitcast.66), channel_id=1, replica_groups=mesh['ctx'=16,'head'=8] {'ctx'}, dimensions={0}, use_global_device_ids=true | all-gather | bytes 139264 | tf_op jit(solution)/shard_map/all_gather | solution.py:21
  32.7 189.0 %while.15 = (s32[]{:T(128)}, f32[1,512]{1,0:T(1,128)S(1)}, f32[1,512]{1,0:T(1,128)S(1)}, f32[1,512,128]{2,1,0:T(8,128)S(1)}, s32[16]{0:T(128)S(1)}, /*index=5*/s...) while((s32[]{:T(128)}, f32[1,512]{1,0:T(1,128)S(1)}, ...), condition=%wide.region_3.4_spmd.clone, body=%wide.region_0.3_spmd.clone.sunk | while | flops 545460736 | bytes 31121916 | solution.py:60
  35.4 3.7 fusion.46
  47.2 3.7 fusion.46
  59.0 3.7 fusion.46
  70.9 3.7 fusion.46
  82.7 3.7 fusion.46
  94.5 3.7 fusion.46
  106.3 3.7 fusion.46
  118.1 3.7 fusion.46
  129.9 3.7 fusion.46
  141.7 3.7 fusion.46
  153.6 3.7 fusion.46
  165.4 3.7 fusion.46
  177.2 3.7 fusion.46
  189.0 3.7 fusion.46
  200.8 3.7 fusion.46
  223.0 72.1 %pmax.7 = f32[64,8]{1,0:T(8,128)S(1)} all-reduce(f32[64,8]{1,0:T(8,128)S(1)} %reshape_transpose_reshape.14), channel_id=1, replica_groups=mesh['ctx'=16,'head'=8] {'ctx'}, use_global_device_ids=true, to_apply=%region_4.5 | all-reduce | flops 512 | bytes 4096 | tf_op jit(solution)/shard_map/pmax | solution.py:75
  296.8 69.5 %psum.43 = f32[64,8]{1,0:T(8,128)S(1)} all-reduce(f32[64,8]{1,0:T(8,128)S(1)} %get-tuple-element.120), channel_id=1, replica_groups=mesh['ctx'=16,'head'=8] {'ctx'}, use_global_device_ids=true, to_apply=%region_6.7 | all-reduce | flops 512 | bytes 4096 | tf_op jit(solution)/shard_map/psum | solution.py:77
  366.3 12.1 %all-reduce.6.cloned.1.call-done = f32[64,8,128]{2,1,0:T(8,128)} async-done(((f32[64,8,128]{2,1,0:T(8,128)}), f32[64,8,128]{2,1,0:T(8,128)}) %all-reduce.6.cloned.1.call-update) | async-done | bytes 262160 | tf_op jit(solution)/shard_map/psum | solution.py:77
  380.5 57.5 %all-reduce.8.cloned.1.call-done = f32[64,320]{1,0:T(8,128)} async-done(((f32[64,320]{1,0:T(8,128)}), f32[64,320]{1,0:T(8,128)}) %all-reduce.8.cloned.1.call-update) | async-done | bytes 81936 | tf_op jit(solution)/shard_map/psum | solution.py:87
  446.1 40.6 %psum.45 = f32[64]{0:T(128)S(1)} all-reduce(f32[64]{0:T(128)S(1)} %get-tuple-element.124), channel_id=1, replica_groups=mesh['ctx'=16,'head'=8] {'ctx'}, use_global_device_ids=true, to_apply=%region_9.10 | all-reduce | flops 64 | bytes 512 | tf_op jit(solution)/shard_map/psum | solution.py:94
  486.7 45.5 %all-reduce.10.cloned.1.call-done = (f32[64,3200]{1,0:T(8,128)}, f32[64,3200]{1,0:T(8,128)}) async-done(((f32[64,3200]{1,0:T(8,128)}, f32[64,3200]{1,0:T(8,128)}), (f32[64,3200]{1,0:T(8,128)}, f32[64,3200]{1,0:T(8,128)})) %all-reduce.10.cloned.1.call-update) | async-done | bytes 1638416 | tf_op jit(solution)/shard_map/psum | solution.py:95
  535.1 25.0 %all-reduce = bf16[64,320]{1,0:T(8,128)(2,1)S(1)} all-reduce(f32[64,320]{1,0:T(8,128)S(1)} %fusion.23), channel_id=2, replica_groups=mesh['ctx'=16,'head'=8] {'head'}, use_global_device_ids=true, to_apply=%region_12.13.clone | all-reduce | flops 20480 | bytes 122880
  (216 shorter events, 128.0 us)
Async XLA Ops:
  7.2 432.5 %copy-start = (bf16[320,3200]{1,0:T(8,128)(2,1)S(1)}, bf16[320,3200]{1,0:T(8,128)(2,1)}, u32[]{:S(2)}) copy-start(bf16[320,3200]{1,0:T(8,128)(2,1)} %param.21) | copy-start | bytes 6144004
  7.2 371.2 %all-reduce.6.cloned.1.call-start = ((), (), s32[]{:S(2)}) async-start(), calls=%async_computation | async-start | bytes 524288 | tf_op jit(solution)/shard_map/psum | solution.py:77
  32.6 346.8 %copy-start.2 = (bf16[1024,320]{0,1:T(8,128)(2,1)S(1)}, bf16[1024,320]{0,1:T(8,128)(2,1)}, u32[]{:S(2)}) copy-start(bf16[1024,320]{0,1:T(8,128)(2,1)} %param.19) | copy-start | bytes 1966084
  32.6 405.4 %copy-start.3 = (bf16[64,320]{1,0:T(8,128)(2,1)S(1)}, bf16[64,320]{1,0:T(8,128)(2,1)}, u32[]{:S(2)}) copy-start(bf16[64,320]{1,0:T(8,128)(2,1)} %param.18) | copy-start | bytes 122884
  32.6 405.4 %copy-start.4 = (f32[320]{0:T(512)S(1)}, f32[320]{0:T(512)}, u32[]{:S(2)}) copy-start(f32[320]{0:T(512)} %param.20) | copy-start | bytes 3844
  39.1 3.4 copy-start.1
  50.9 3.4 copy-start.1
  62.7 3.4 copy-start.1
  74.5 3.4 copy-start.1
  86.4 3.4 copy-start.1
  98.2 3.4 copy-start.1
  110.0 3.4 copy-start.1
  121.8 3.4 copy-start.1
  133.6 3.4 copy-start.1
  145.4 3.4 copy-start.1
  157.2 3.4 copy-start.1
  169.1 3.4 copy-start.1
  180.9 3.4 copy-start.1
  192.7 3.4 copy-start.1
  204.5 3.4 copy-start.1
  216.3 3.4 copy-start.1
  296.7 141.3 %all-reduce.8.cloned.1.call-start = ((), (), s32[]{:S(2)}) async-start(), calls=%async_computation.1 | async-start | bytes 196608 | tf_op jit(solution)/shard_map/psum | solution.py:87
  379.5 64.7 %copy-start.5 = (u32[128]{0:T(128)S(1)}, u32[128]{0:T(128)}, u32[]{:S(2)}) copy-start(u32[128]{0:T(128)} %constant.51) | copy-start | bytes 1540
  380.5 151.8 %all-reduce.10.cloned.1.call-start = ((), (), s32[]{:S(2)}) async-start(), calls=%async_computation.2 | async-start | bytes 3276800 | tf_op jit(solution)/shard_map/psum | solution.py:95
Sparse Core Ops, SparseCore 0:
  296.8 81.4 all-reduce.5
  380.7 57.2 all-reduce.7
  444.3 87.9 all-reduce.9
where the time goes:
time: 570 us; the launch traced here: 567 us
  blocking collectives  233 us (41%)
  waiting for transfers between devices  115 us (20%)
  matrix products  98 us (17%)
  other arithmetic  52.9 us (9%)
  local copies, waits for them, and re-layouts  32.3 us (6%)
  loops' own time  21.6 us (4%)
  between operations  14.6 us (3%)
    pmax x1, blocking collectives, local(): top_score = lax.pmax(row_high, 'ctx')  72.1 us
    psum x1, blocking collectives, local(): lax.psum((row_acc * rescale[:, :, None], row_total * rescale), 'ctx')  69.5 us
    dot_general x16, matrix products, visit(): jnp.einsum('hrd,khd->hrk', query_heads, key_block, preferred_element_type...  59.1 us
    psum x1, waiting for transfers between devices, local(): mixed = lax.psum(projected, 'head')  57.5 us
    reduce_sum x16, other arithmetic, visit(): row_total = row_total * rescale + jnp.sum(weights, axis=2)  47.5 us
    psum x1, waiting for transfers between devices, local(): gate, upward = lax.psum((gate_part, up_part), 'ctx')  45.5 us
    psum x1, blocking collectives, local(): square_total = lax.psum(squares, 'ctx')  40.6 us
    dot_general x16, matrix products, visit(): jnp.einsum('hrk,khd->hrd', weights.astype(jnp.bfloat16), value_block, pre...  30.7 us
  transfers between devices with their start and end apart: 3, of which 3 were waited for; matrix products, arithmetic and copies ran while one was open for 0% of the time, Pallas kernels for 0%

commit v1 on v0

--- a/solution.py
+++ b/solution.py
@@ -84,7 +84,7 @@
         whole_rows, lax.axis_index("ctx") * rows_local, rows_local, 0
     )
     projected = jnp.dot(whole_rows, wo, preferred_element_type=jnp.float32)
-    mixed = lax.psum(projected, "head")
+    mixed = jnp.sum(lax.all_gather(projected, "head"), axis=0)
     combined = residual.astype(jnp.float32) + mixed
     stream = combined.astype(jnp.bfloat16)
     squares = jnp.sum(combined * combined, axis=1)

time: 570 us -> 524 us (0.919)
  waiting for transfers between devices: 115 us -> 59.6 us
  blocking collectives: 233 us -> 244 us
    psum x1 -> x0, waiting for transfers between devices: 57.5 us -> none  [local(): mixed = lax.psum(projected, 'head')]
    all_gather x0 -> x1, blocking collectives: none -> 13.7 us  [local(): mixed = jnp.sum(lax.all_gather(projected, 'head'), axis=0)]
  transfers between devices with their start and end apart: 3 -> 2, of which waited for: 3 -> 2; matrix products, arithmetic and copies ran while one was open for 0% -> 0% of each run, Pallas kernels for 0% -> 0%
where the time goes in v1:
time: 524 us; the launch traced here: 522 us
  blocking collectives  244 us (47%)
  matrix products  97.4 us (19%)
  waiting for transfers between devices  59.6 us (11%)
  other arithmetic  52.1 us (10%)
  local copies, waits for them, and re-layouts  32.3 us (6%)
  loops' own time  21.6 us (4%)
  between operations  14.9 us (3%)
    pmax x1, blocking collectives, local(): top_score = lax.pmax(row_high, 'ctx')  72.1 us
    psum x1, blocking collectives, local(): lax.psum((row_acc * rescale[:, :, None], row_total * rescale), 'ctx')  69.5 us
    dot_general x16, matrix products, visit(): jnp.einsum('hrd,khd->hrk', query_heads, key_block, preferred_element_type...  59.1 us
    psum x1, waiting for transfers between devices, local(): gate, upward = lax.psum((gate_part, up_part), 'ctx')  47.5 us
    reduce_sum x16, other arithmetic, visit(): row_total = row_total * rescale + jnp.sum(weights, axis=2)  47.5 us
    psum x1, blocking collectives, local(): square_total = lax.psum(squares, 'ctx')  38.2 us
    dot_general x16, matrix products, visit(): jnp.einsum('hrk,khd->hrd', weights.astype(jnp.bfloat16), value_block, pre...  30.7 us
    all_gather x1, blocking collectives, local(): everyone = lax.all_gather(queries, 'ctx', axis=0, tiled=True)  25.3 us
  transfers between devices with their start and end apart: 2, of which 2 were waited for; matrix products, arithmetic and copies ran while one was open for 0% of the time, Pallas kernels for 0%

profile of v1, /device:TPU:0, one launch (start us, length us, event | category | flops | bytes accessed | tf_op | source)
XLA Modules:
  0.0 521.8 jit_solution(4104244788385465611)
XLA Ops:
  7.3 25.3 %all-gather.1 = bf16[16,4,1024]{2,1,0:T(4,128)(2,1)S(1)} all-gather(bf16[1,4,1024]{2,1,0:T(4,128)(2,1)} %bitcast.68), channel_id=1, replica_groups=mesh['ctx'=16,'head'=8] {'ctx'}, dimensions={0}, use_global_device_ids=true | all-gather | bytes 139264 | tf_op jit(solution)/shard_map/all_gather | solution.py:21
  32.6 189.1 %while.15 = (s32[]{:T(128)}, f32[1,512]{1,0:T(1,128)S(1)}, f32[1,512]{1,0:T(1,128)S(1)}, f32[1,512,128]{2,1,0:T(8,128)S(1)}, s32[16]{0:T(128)S(1)}, /*index=5*/s...) while((s32[]{:T(128)}, f32[1,512]{1,0:T(1,128)S(1)}, ...), condition=%wide.region_3.4_spmd.clone, body=%wide.region_0.3_spmd.clone.sunk | while | flops 545460736 | bytes 31121916 | solution.py:60
  35.4 3.7 fusion.46
  47.2 3.7 fusion.46
  59.0 3.7 fusion.46
  70.8 3.7 fusion.46
  82.6 3.7 fusion.46
  94.5 3.7 fusion.46
  106.3 3.7 fusion.46
  118.1 3.7 fusion.46
  129.9 3.7 fusion.46
  141.7 3.7 fusion.46
  153.5 3.7 fusion.46
  165.4 3.7 fusion.46
  177.2 3.7 fusion.46
  189.0 3.7 fusion.46
  212.6 3.7 fusion.46
  223.0 72.1 %pmax.7 = f32[64,8]{1,0:T(8,128)S(1)} all-reduce(f32[64,8]{1,0:T(8,128)S(1)} %reshape_transpose_reshape.14), channel_id=1, replica_groups=mesh['ctx'=16,'head'=8] {'ctx'}, use_global_device_ids=true, to_apply=%region_4.5 | all-reduce | flops 512 | bytes 4096 | tf_op jit(solution)/shard_map/pmax | solution.py:75
  296.7 69.5 %psum.36 = f32[64,8]{1,0:T(8,128)S(1)} all-reduce(f32[64,8]{1,0:T(8,128)S(1)} %get-tuple-element.120), channel_id=1, replica_groups=mesh['ctx'=16,'head'=8] {'ctx'}, use_global_device_ids=true, to_apply=%region_6.7 | all-reduce | flops 512 | bytes 4096 | tf_op jit(solution)/shard_map/psum | solution.py:77
  366.3 12.1 %all-reduce.5.cloned.1.call-done = f32[64,8,128]{2,1,0:T(8,128)} async-done(((f32[64,8,128]{2,1,0:T(8,128)}), f32[64,8,128]{2,1,0:T(8,128)}) %all-reduce.5.cloned.1.call-update) | async-done | bytes 262160 | tf_op jit(solution)/shard_map/psum | solution.py:77
  379.8 13.7 %all-gather = f32[512,320]{1,0:T(8,128)S(1)} all-gather(f32[64,320]{1,0:T(8,128)S(1)} %fusion.26), channel_id=2, replica_groups=mesh['ctx'=16,'head'=8] {'head'}, dimensions={0}, use_global_device_ids=true | all-gather | bytes 737280 | tf_op jit(solution)/shard_map/all_gather | solution.py:87
  400.1 38.2 %psum.37 = f32[64]{0:T(128)S(1)} all-reduce(f32[64]{0:T(128)S(1)} %get-tuple-element.124), channel_id=1, replica_groups=mesh['ctx'=16,'head'=8] {'ctx'}, use_global_device_ids=true, to_apply=%region_9.10 | all-reduce | flops 64 | bytes 512 | tf_op jit(solution)/shard_map/psum | solution.py:94
  438.9 47.5 %all-reduce.7.cloned.1.call-done = (f32[64,3200]{1,0:T(8,128)}, f32[64,3200]{1,0:T(8,128)}) async-done(((f32[64,3200]{1,0:T(8,128)}, f32[64,3200]{1,0:T(8,128)}), (f32[64,3200]{1,0:T(8,128)}, f32[64,3200]{1,0:T(8,128)})) %all-reduce.7.cloned.1.call-update) | async-done | bytes 1638416 | tf_op jit(solution)/shard_map/psum | solution.py:95
  489.3 25.0 %all-reduce = bf16[64,320]{1,0:T(8,128)(2,1)S(1)} all-reduce(f32[64,320]{1,0:T(8,128)S(1)} %fusion.23), channel_id=3, replica_groups=mesh['ctx'=16,'head'=8] {'head'}, use_global_device_ids=true, to_apply=%region_12.13.clone | all-reduce | flops 20480 | bytes 122880
  (215 shorter events, 126.5 us)
Async XLA Ops:
  7.2 387.2 %copy-start = (bf16[320,3200]{1,0:T(8,128)(2,1)S(1)}, bf16[320,3200]{1,0:T(8,128)(2,1)}, u32[]{:S(2)}) copy-start(bf16[320,3200]{1,0:T(8,128)(2,1)} %param.21) | copy-start | bytes 6144004
  7.2 371.2 %all-reduce.5.cloned.1.call-start = ((), (), s32[]{:S(2)}) async-start(), calls=%async_computation | async-start | bytes 524288 | tf_op jit(solution)/shard_map/psum | solution.py:77
  32.6 346.8 %copy-start.2 = (bf16[1024,320]{0,1:T(8,128)(2,1)S(1)}, bf16[1024,320]{0,1:T(8,128)(2,1)}, u32[]{:S(2)}) copy-start(bf16[1024,320]{0,1:T(8,128)(2,1)} %param.19) | copy-start | bytes 1966084
  39.1 3.4 copy-start.1
  50.9 3.4 copy-start.1
  62.7 3.4 copy-start.1
  74.5 3.4 copy-start.1
  86.3 3.4 copy-start.1
  98.2 3.4 copy-start.1
  110.0 3.4 copy-start.1
  121.8 3.4 copy-start.1
  133.6 3.4 copy-start.1
  145.4 3.4 copy-start.1
  157.2 3.4 copy-start.1
  169.0 3.4 copy-start.1
  180.9 3.4 copy-start.1
  192.7 3.4 copy-start.1
  204.5 3.4 copy-start.1
  216.3 3.4 copy-start.1
  221.7 171.9 %copy-start.3 = (bf16[64,320]{1,0:T(8,128)(2,1)S(1)}, bf16[64,320]{1,0:T(8,128)(2,1)}, u32[]{:S(2)}) copy-start(bf16[64,320]{1,0:T(8,128)(2,1)} %param.18) | copy-start | bytes 122884
  221.7 171.9 %copy-start.4 = (f32[320]{0:T(512)S(1)}, f32[320]{0:T(512)}, u32[]{:S(2)}) copy-start(f32[320]{0:T(512)} %param.20) | copy-start | bytes 3844
  296.7 189.8 %all-reduce.7.cloned.1.call-start = ((), (), s32[]{:S(2)}) async-start(), calls=%async_computation.1 | async-start | bytes 3276800 | tf_op jit(solution)/shard_map/psum | solution.py:95
  393.5 5.3 %copy-start.5 = (u32[128]{0:T(128)S(1)}, u32[128]{0:T(128)}, u32[]{:S(2)}) copy-start(u32[128]{0:T(128)} %constant.51) | copy-start | bytes 1540
Sparse Core Ops, SparseCore 0:
  296.8 81.4 all-reduce.4
  399.0 87.4 all-reduce.6
